TPU v7x, 32 devices: a whole 2x2x4 slice. The times are simulated.
32 devices in a mesh: row: 2 (over y), col: 16 (over z, x, core).
Axes of the slice: x: 2, y: 2, z: 4, core: 2. Of those that a mesh axis runs over, the one named last changes fastest.
Arguments:
- start_block: float32 [32, 8192], P(None, 'col'), may hold values from -6 to 6
- energies: float32 [8192], P('col'), may hold values from 1 to 10
- hamiltonian: float32 [16, 16, 512, 512], P('row', 'col'), may hold values from -0.125 to 0.125
Outputs:
- recurrence: float32 [2, 2, 32, 32], replicated
- next_block: float32 [32, 8192], P(None, 'col')
All inputs are finite; a program needn't handle non-finite values.
Results may differ from a plain program's by a relative error of at most 0.0003.
Values sent between devices are 32-bit elements; how exact they have to be, the bound alone decides.
A program may use at most 64 MiB of HBM per device.

v0:
```python
import jax
import jax.numpy as jnp
from jax import lax
from jax.sharding import PartitionSpec as P

ITERS = 2
FULL_PRECISION = lax.Precision.HIGHEST


def mean_inner(left, right):
    length = lax.axis_size("col") * left.shape[1]
    return lax.psum(jnp.dot(left, right.T, precision=FULL_PRECISION), "col") / length


def normalize(block):
    factor = jnp.linalg.cholesky(mean_inner(block, block))
    return (lax.linalg.triangular_solve(factor, block, left_side=True, lower=True), factor)


def on_device(start_block, energies, hamiltonian):
    row_index = lax.axis_index("row")
    col_index = lax.axis_index("col")
    row_count = lax.axis_size("row")
    col_count = lax.axis_size("col")
    slot_count = hamiltonian.shape[0]
    width = hamiltonian.shape[2]
    vec_count = start_block.shape[0]
    blocks = hamiltonian[:, 0]
    block_rows = row_index + row_count * jnp.arange(slot_count, dtype=jnp.int32)
    weight = jnp.where(
        block_rows < col_index,
        jnp.float32(1.0),
        jnp.where(block_rows == col_index, jnp.float32(0.5), jnp.float32(0.0)),
    )
    selector = (block_rows[:, None] == jnp.arange(col_count, dtype=jnp.int32)[None, :]).astype(
        jnp.float32
    )
    current, factor = normalize(start_block)
    previous = jnp.zeros_like(current)
    last_factor = jnp.zeros((vec_count, vec_count), jnp.float32)
    history = []
    for iteration in range(ITERS):
        whole = lax.all_gather(current, "col", axis=1, tiled=True).reshape(
            vec_count, col_count, width
        )
        chosen = jnp.take(whole, block_rows, axis=1) * weight[None, :, None]
        downward = jnp.einsum("psk,skl->pl", chosen, blocks, precision=FULL_PRECISION)
        across = (
            jnp.einsum("pl,skl->spk", current, blocks, precision=FULL_PRECISION)
            * weight[:, None, None]
        )
        spread = jnp.einsum("sj,spk->pjk", selector, across, precision=FULL_PRECISION).reshape(
            vec_count, col_count * width
        )
        mine = lax.psum_scatter(spread, "col", scatter_dimension=1, tiled=True)
        column_total = lax.psum(downward + mine, "row")
        residual_block = (
            column_total
            + energies[None, :] * current
            - jnp.dot(last_factor.T, previous, precision=FULL_PRECISION)
        )
        diagonal_block = mean_inner(residual_block, current)
        residual_block = residual_block - jnp.dot(diagonal_block, current, precision=FULL_PRECISION)
        following, new_factor = normalize(residual_block)
        history.append(jnp.stack([diagonal_block, new_factor]))
        previous, current, last_factor = (current, following, new_factor)
    return (jnp.stack(history), current)


def solution(mesh):
    placed = (P(None, "col"), P("col"), P("row", "col", None, None))
    return jax.shard_map(
        on_device, mesh=mesh, in_specs=placed, out_specs=(P(), P(None, "col")), check_vma=False
    )
```

profile of v0, /device:TPU:0, one launch (start us, length us, event | category | flops | bytes accessed | tf_op | source)
XLA Modules:
  0.0 588.7 jit_solution(12538500507345331128)
XLA Ops:
  7.2 0.0 all-gather.3.cloned.1.call-start
  7.2 0.8 copy-done
  8.0 0.2 fusion.79
  8.2 63.0 %psum.49 = f32[32,32]{1,0:T(8,128)S(1)} all-reduce(f32[32,32]{1,0:T(8,128)S(1)} %fusion.79), channel_id=1, replica_groups=mesh['row'=2,'col'=16] {'col'}, use_global_device_ids=true, to_apply=%region_0.1 | all-reduce | flops 1024 | bytes 8192 | tf_op jit(solution)/shard_map/psum | solution.py:12
  71.2 0.1 copy.13
  71.3 0.1 copy.14
  71.3 2.9 cholesky.59
  74.3 0.6 compare_reduce_fusion.2
  74.9 0.7 fusion.47
  75.6 2.5 custom-call.7
  78.0 0.9 fusion.54
  78.9 0.0 all-gather.3.cloned.1.call-update
  79.0 0.0 reduce-scatter.3.cloned.1.call-start
  79.0 10.0 %fusion.11 = f32[8,32,512]{2,1,0:T(8,128)S(1)} fusion(f32[8,1,512,512]{3,2,1,0:T(8,128)} %param.10, f32[8]{0:T(128)S(1)} %compare_select_fusion.2, f32[32,512]{1,0:T(8,128)} %fusion.54), kind=kOutput, calls=%fused_computation.11 | convolution fusion | flops 805437440 | bytes 8978464 | tf_op jit(solution)/shard_map/pl,skl->spk/dot_general | solution.py:49
  89.0 0.9 fusion.34
  89.9 1.6 copy.25
  91.6 0.0 reduce-scatter.3.cloned.1.call-update
  91.6 0.0 all-reduce.3.cloned.1.call-start
  91.7 22.6 %all-gather.3.cloned.1.call-done = f32[32,8192]{1,0:T(8,128)} async-done(((f32[32,512]{1,0:T(8,128)}), f32[32,8192]{1,0:T(8,128)}) %all-gather.3.cloned.1.call-update) | async-done | bytes 1048592 | tf_op jit(solution)/shard_map/all_gather | solution.py:43
  114.3 1.3 copy.34
  115.6 0.6 gather_fusion
  116.2 58.3 %reduce-scatter.3.cloned.1.call-done = f32[32,512]{1,0:T(8,128)} async-done(((f32[32,8192]{1,0:T(8,128)}), f32[32,512]{1,0:T(8,128)}) %reduce-scatter.3.cloned.1.call-update) | async-done | bytes 65552 | tf_op jit(solution)/shard_map/reduce_scatter | solution.py:55
  174.5 7.8 %fusion.29 = f32[32,512]{1,0:T(8,128)} fusion(f32[32,512]{1,0:T(8,128)} %reduce-scatter.3.cloned.1.call-done, f32[8,1,512,512]{3,2,1,0:T(8,128)} %param.10, f32[8,32,512]{2,1,0:T(8,128)S(1)} %gather_fusion, f32[8]{0:T(128)S(1)} %compare_select_fusion.2, pred[8]{0:T(512)(128)(4,1)S(1)} %compare_and_fusion), kind=kOutput, calls=%fused_computation.21 | convolution fusion | flops 805584896 | bytes 9044008 | tf_op jit(solution)/shard_map/psk,skl->pl/dot_general | solution.py:47
  182.3 0.0 all-reduce.3.cloned.1.call-update
  182.3 0.0 all-gather.5.cloned.1.call-start
  182.4 20.1 %all-reduce.3.cloned.1.call-done = f32[32,512]{1,0:T(8,128)} async-done(((f32[32,512]{1,0:T(8,128)}), f32[32,512]{1,0:T(8,128)}) %all-reduce.3.cloned.1.call-update) | async-done | bytes 65552 | tf_op jit(solution)/shard_map/psum | solution.py:56
  202.5 1.0 convolution_subtract_fusion.3
  203.5 0.2 fusion.80
  203.7 60.7 %psum.51 = f32[32,32]{1,0:T(8,128)S(1)} all-reduce(f32[32,32]{1,0:T(8,128)S(1)} %fusion.80), channel_id=1, replica_groups=mesh['row'=2,'col'=16] {'col'}, use_global_device_ids=true, to_apply=%region_5.9 | all-reduce | flops 1024 | bytes 8192 | tf_op jit(solution)/shard_map/psum | solution.py:12
  264.5 0.2 convolution_subtract_fusion.2
  264.7 0.2 fusion.81
  264.9 57.6 %psum.52 = f32[32,32]{1,0:T(8,128)S(1)} all-reduce(f32[32,32]{1,0:T(8,128)S(1)} %fusion.81), channel_id=1, replica_groups=mesh['row'=2,'col'=16] {'col'}, use_global_device_ids=true, to_apply=%region_6.10 | all-reduce | flops 1024 | bytes 8192 | tf_op jit(solution)/shard_map/psum | solution.py:12
  322.5 0.1 copy.17
  322.6 0.1 copy.18
  322.6 2.9 cholesky.70
  325.6 0.7 compare_reduce_fusion.1
  326.3 0.6 fusion.60
  326.9 2.5 custom-call.8
  329.4 0.9 fusion.51
  330.3 0.2 reduce-scatter.5.cloned.1.call-start
  330.5 10.0 %fusion.17 = f32[8,32,512]{2,1,0:T(8,128)S(1)} fusion(f32[8,1,512,512]{3,2,1,0:T(8,128)} %param.10, f32[8]{0:T(128)S(1)} %compare_select_fusion.2, f32[32,512]{1,0:T(8,128)} %fusion.51), kind=kOutput, calls=%fused_computation.13 | convolution fusion | flops 805437440 | bytes 8978464 | tf_op jit(solution)/shard_map/pl,skl->spk/dot_general | solution.py:49
  340.5 0.9 fusion.32
  341.4 1.6 copy.26
  343.1 0.0 all-reduce.5.cloned.1.call-start
  343.1 21.5 %all-gather.5.cloned.1.call-done = f32[32,8192]{1,0:T(8,128)} async-done(((f32[32,512]{1,0:T(8,128)}), f32[32,8192]{1,0:T(8,128)}) %all-gather.5.cloned.1.call-update) | async-done | bytes 1048592 | tf_op jit(solution)/shard_map/all_gather | solution.py:43
  364.6 1.3 copy.33
  366.0 0.6 gather_fusion.1
  366.5 58.2 %reduce-scatter.5.cloned.1.call-done = f32[32,512]{1,0:T(8,128)} async-done(((f32[32,8192]{1,0:T(8,128)}), f32[32,512]{1,0:T(8,128)}) %reduce-scatter.5.cloned.1.call-update) | async-done | bytes 65552 | tf_op jit(solution)/shard_map/reduce_scatter | solution.py:55
  424.7 7.8 %fusion.26 = f32[32,512]{1,0:T(8,128)} fusion(f32[32,512]{1,0:T(8,128)} %reduce-scatter.5.cloned.1.call-done, f32[8,1,512,512]{3,2,1,0:T(8,128)} %param.10, f32[8,32,512]{2,1,0:T(8,128)S(1)} %gather_fusion.1, f32[8]{0:T(128)S(1)} %compare_select_fusion.2, pred[8]{0:T(512)(128)(4,1)S(1)} %compare_and_fusion), kind=kOutput, calls=%fused_computation.20 | convolution fusion | flops 805584896 | bytes 9044008 | tf_op jit(solution)/shard_map/psk,skl->pl/dot_general | solution.py:47
  432.6 20.2 %all-reduce.5.cloned.1.call-done = f32[32,512]{1,0:T(8,128)} async-done(((f32[32,512]{1,0:T(8,128)}), f32[32,512]{1,0:T(8,128)}) %all-reduce.5.cloned.1.call-update) | async-done | bytes 65552 | tf_op jit(solution)/shard_map/psum | solution.py:56
  452.7 1.7 convolution_subtract_fusion.1
  454.5 0.2 fusion.82
  454.7 60.7 %psum.54 = f32[32,32]{1,0:T(8,128)S(1)} all-reduce(f32[32,32]{1,0:T(8,128)S(1)} %fusion.82), channel_id=1, replica_groups=mesh['row'=2,'col'=16] {'col'}, use_global_device_ids=true, to_apply=%region_9.13 | all-reduce | flops 1024 | bytes 8192 | tf_op jit(solution)/shard_map/psum | solution.py:12
  515.4 0.2 convolution_subtract_fusion
  515.6 0.2 fusion.83
  515.8 57.6 %psum.55 = f32[32,32]{1,0:T(8,128)S(1)} all-reduce(f32[32,32]{1,0:T(8,128)S(1)} %fusion.83), channel_id=1, replica_groups=mesh['row'=2,'col'=16] {'col'}, use_global_device_ids=true, to_apply=%region_10.14 | all-reduce | flops 1024 | bytes 8192 | tf_op jit(solution)/shard_map/psum | solution.py:12
  573.4 0.1 copy.21
  573.5 0.1 copy.22
  573.6 2.9 cholesky.81
  576.5 0.6 compare_reduce_fusion
  577.2 0.7 select_bitcast_fusion
  577.9 2.4 custom-call.9
  580.3 0.9 fusion.48
  581.2 0.6 pad_maximum_fusion
  (28 shorter events, 0.3 us)
Async XLA Ops:
  7.2 0.8 copy-start
  7.2 107.1 %all-gather.3.cloned.1.call-start = ((), (), s32[]{:S(2)}) async-start(), calls=%async_computation.2 | async-start | bytes 1114112 | tf_op jit(solution)/shard_map/all_gather | solution.py:43
  79.0 95.5 %reduce-scatter.3.cloned.1.call-start = ((), (), s32[]{:S(2)}) async-start(), calls=%async_computation.3 | async-start | bytes 1114112 | tf_op jit(solution)/shard_map/reduce_scatter | solution.py:55
  89.0 113.5 %copy-start.1 = (f32[32,512]{1,0:T(8,128)S(1)}, f32[32,512]{1,0:T(8,128)}, u32[]{:S(2)}) copy-start(f32[32,512]{1,0:T(8,128)} %fusion.54) | copy-start | bytes 196612
  89.0 113.5 %copy-start.3 = (f32[512]{0:T(512)S(1)}, f32[512]{0:T(512)}, u32[]{:S(2)}) copy-start(f32[512]{0:T(512)} %param.9) | copy-start | bytes 6148
  91.6 110.9 %all-reduce.3.cloned.1.call-start = ((), (), s32[]{:S(2)}) async-start(), calls=%async_computation.4 | async-start | bytes 131072 | tf_op jit(solution)/shard_map/psum | solution.py:56
  182.3 182.3 %all-gather.5.cloned.1.call-start = ((), (), s32[]{:S(2)}) async-start(), calls=%async_computation.5 | async-start | bytes 1114112 | tf_op jit(solution)/shard_map/all_gather | solution.py:43
  330.3 94.4 %reduce-scatter.5.cloned.1.call-start = ((), (), s32[]{:S(2)}) async-start(), calls=%async_computation.6 | async-start | bytes 1114112 | tf_op jit(solution)/shard_map/reduce_scatter | solution.py:55
  340.5 112.2 %copy-start.2 = (f32[32,512]{1,0:T(8,128)S(1)}, f32[32,512]{1,0:T(8,128)}, u32[]{:S(2)}) copy-start(f32[32,512]{1,0:T(8,128)} %fusion.51) | copy-start | bytes 196612
  343.1 109.7 %all-reduce.5.cloned.1.call-start = ((), (), s32[]{:S(2)}) async-start(), calls=%async_computation.7 | async-start | bytes 131072 | tf_op jit(solution)/shard_map/psum | solution.py:56
Sparse Core Ops, SparseCore 0:
  79.1 35.1 all-gather.2
  117.9 56.5 reduce-scatter.2
  182.5 20.0 all-reduce.2
  330.4 34.1 all-gather.4
  368.1 56.5 reduce-scatter.4
  432.7 20.0 all-reduce.4
where the time goes:
time: 589 us
  blocking collectives  300 us (51%)
  waiting for transfers between devices  201 us (34%)
  matrix products  44 us (7%)
  other arithmetic  20.9 us (4%)
  between operations  14.4 us (2%)
  local copies, waits for them, and re-layouts  8.33 us (1%)
    psum x5, blocking collectives, mean_inner(): lax.psum(jnp.dot(left, right.T, precision=FULL_PRECISION), 'col') / length  300 us
    reduce_scatter x2, waiting for transfers between devices, on_device(): mine = lax.psum_scatter(spread, 'col', scatter_dimension=1, tiled=True)  117 us
    all_gather x2, waiting for transfers between devices, on_device(): lax.all_gather(current, 'col', axis=1, tiled=True)  44.1 us
    psum x2, waiting for transfers between devices, on_device(): column_total = lax.psum(downward + mine, 'row')  40.3 us
    dot_general x2, matrix products, on_device(): jnp.einsum('pl,skl->spk', current, blocks, precision=FULL_PRECISION)  19.9 us
    dot_general x2, matrix products, on_device(): jnp.einsum('psk,skl->pl', chosen, blocks, precision=FULL_PRECISION)  15.6 us
  transfers between devices with their start and end apart: 6, of which 6 were waited for; matrix products, arithmetic and copies ran while one was open for 5% of the time, Pallas kernels for 0%

commit v1 on v0

--- a/solution.py
+++ b/solution.py
@@ -53,7 +53,7 @@
             vec_count, col_count * width
         )
         mine = lax.psum_scatter(spread, "col", scatter_dimension=1, tiled=True)
-        column_total = lax.psum(downward + mine, "row")
+        column_total = jnp.sum(lax.all_gather(downward + mine, "row"), axis=0)
         residual_block = (
             column_total
             + energies[None, :] * current

time: 589 us -> 550 us (0.934)
  waiting for transfers between devices: 201 us -> 162 us
    psum x2 -> x0, waiting for transfers between devices: 40.3 us -> none  [on_device(): column_total = lax.psum(downward + mine, 'row')]
    all_gather x0 -> x2, blocking collectives: none -> 9.87 us  [on_device(): column_total = jnp.sum(lax.all_gather(downward + mine, 'row'), axis=0)]
    psum x5, blocking collectives: 300 us -> 293 us  [mean_inner(): lax.psum(jnp.dot(left, right.T, precision=FULL_PRECISION), 'col') / length]
  transfers between devices with their start and end apart: 6 -> 4, of which waited for: 6 -> 4; matrix products, arithmetic and copies ran while one was open for 5% -> 5% of each run, Pallas kernels for 0% -> 0%
where the time goes in v1:
time: 550 us
  blocking collectives  303 us (55%)
  waiting for transfers between devices  162 us (29%)
  matrix products  41.2 us (7%)
  other arithmetic  20.9 us (4%)
  between operations  14.1 us (3%)
  local copies, waits for them, and re-layouts  8.33 us (2%)
    psum x5, blocking collectives, mean_inner(): lax.psum(jnp.dot(left, right.T, precision=FULL_PRECISION), 'col') / length  293 us
    reduce_scatter x2, waiting for transfers between devices, on_device(): mine = lax.psum_scatter(spread, 'col', scatter_dimension=1, tiled=True)  117 us
    all_gather x2, waiting for transfers between devices, on_device(): lax.all_gather(current, 'col', axis=1, tiled=True)  45.1 us
    dot_general x2, matrix products, on_device(): jnp.einsum('pl,skl->spk', current, blocks, precision=FULL_PRECISION)  19.9 us
    dot_general x2, matrix products, on_device(): jnp.einsum('psk,skl->pl', chosen, blocks, precision=FULL_PRECISION)  14.4 us
  transfers between devices with their start and end apart: 4, of which 4 were waited for; matrix products, arithmetic and copies ran while one was open for 5% of the time, Pallas kernels for 0%

profile of v1, /device:TPU:0, one launch (start us, length us, event | category | flops | bytes accessed | tf_op | source)
XLA Modules:
  0.0 549.7 jit_solution(16072799279525472194)
XLA Ops:
  7.2 0.0 copy-start
  7.2 0.0 all-gather.5.cloned.1.call-start
  7.2 0.8 copy-done
  8.0 0.2 fusion.79
  8.2 63.0 %psum.35 = f32[32,32]{1,0:T(8,128)S(1)} all-reduce(f32[32,32]{1,0:T(8,128)S(1)} %fusion.79), channel_id=1, replica_groups=mesh['row'=2,'col'=16] {'col'}, use_global_device_ids=true, to_apply=%region_0.1 | all-reduce | flops 1024 | bytes 8192 | tf_op jit(solution)/shard_map/psum | solution.py:12
  71.2 0.1 copy.13
  71.3 0.1 copy.14
  71.3 2.9 cholesky.59
  74.3 0.6 compare_reduce_fusion.2
  74.9 0.7 fusion.47
  75.6 2.5 custom-call.7
  78.0 0.9 fusion.54
  78.9 0.0 all-gather.5.cloned.1.call-update
  79.0 0.0 reduce-scatter.3.cloned.1.call-start
  79.0 10.0 %fusion.11 = f32[8,32,512]{2,1,0:T(8,128)S(1)} fusion(f32[8,1,512,512]{3,2,1,0:T(8,128)} %param.10, f32[8]{0:T(128)S(1)} %compare_select_fusion.2, f32[32,512]{1,0:T(8,128)} %fusion.54), kind=kOutput, calls=%fused_computation.11 | convolution fusion | flops 805437440 | bytes 8978464 | tf_op jit(solution)/shard_map/pl,skl->spk/dot_general | solution.py:49
  89.0 0.9 fusion.34
  89.9 1.6 copy.25
  91.6 0.0 reduce-scatter.3.cloned.1.call-update
  91.6 0.0 all-gather.7.cloned.1.call-start
  91.7 22.6 %all-gather.5.cloned.1.call-done = f32[32,8192]{1,0:T(8,128)} async-done(((f32[32,512]{1,0:T(8,128)}), f32[32,8192]{1,0:T(8,128)}) %all-gather.5.cloned.1.call-update) | async-done | bytes 1048592 | tf_op jit(solution)/shard_map/all_gather | solution.py:43
  114.3 1.3 copy.34
  115.6 0.6 gather_fusion
  116.2 58.3 %reduce-scatter.3.cloned.1.call-done = f32[32,512]{1,0:T(8,128)} async-done(((f32[32,8192]{1,0:T(8,128)}), f32[32,512]{1,0:T(8,128)}) %reduce-scatter.3.cloned.1.call-update) | async-done | bytes 65552 | tf_op jit(solution)/shard_map/reduce_scatter | solution.py:55
  174.5 7.2 %fusion.29 = f32[32,512]{1,0:T(8,128)S(1)} fusion(f32[32,512]{1,0:T(8,128)} %reduce-scatter.3.cloned.1.call-done, f32[8,1,512,512]{3,2,1,0:T(8,128)} %param.10, f32[8,32,512]{2,1,0:T(8,128)S(1)} %gather_fusion, f32[8]{0:T(128)S(1)} %compare_select_fusion.2, pred[8]{0:T(512)(128)(4,1)S(1)} %compare_and_fusion), kind=kOutput, calls=%fused_computation.21 | convolution fusion | flops 805584896 | bytes 9044008 | tf_op jit(solution)/shard_map/psk,skl->pl/dot_general | solution.py:47
  181.7 4.9 all-gather
  186.7 0.2 convolution_subtract_fusion.3
  186.8 0.2 fusion.80
  187.0 57.6 %psum.36 = f32[32,32]{1,0:T(8,128)S(1)} all-reduce(f32[32,32]{1,0:T(8,128)S(1)} %fusion.80), channel_id=1, replica_groups=mesh['row'=2,'col'=16] {'col'}, use_global_device_ids=true, to_apply=%region_5.9 | all-reduce | flops 1024 | bytes 8192 | tf_op jit(solution)/shard_map/psum | solution.py:12
  244.7 0.2 convolution_subtract_fusion.2
  244.9 0.2 fusion.81
  245.1 57.6 %psum.37 = f32[32,32]{1,0:T(8,128)S(1)} all-reduce(f32[32,32]{1,0:T(8,128)S(1)} %fusion.81), channel_id=1, replica_groups=mesh['row'=2,'col'=16] {'col'}, use_global_device_ids=true, to_apply=%region_6.10 | all-reduce | flops 1024 | bytes 8192 | tf_op jit(solution)/shard_map/psum | solution.py:12
  302.7 0.1 copy.17
  302.8 0.1 copy.18
  302.8 2.9 cholesky.70
  305.8 0.6 compare_reduce_fusion.1
  306.4 0.7 fusion.60
  307.1 2.5 custom-call.8
  309.6 0.9 fusion.51
  310.4 0.0 all-gather.7.cloned.1.call-update
  310.5 0.2 reduce-scatter.5.cloned.1.call-start
  310.7 10.0 %fusion.17 = f32[8,32,512]{2,1,0:T(8,128)S(1)} fusion(f32[8,1,512,512]{3,2,1,0:T(8,128)} %param.10, f32[8]{0:T(128)S(1)} %compare_select_fusion.2, f32[32,512]{1,0:T(8,128)} %fusion.51), kind=kOutput, calls=%fused_computation.13 | convolution fusion | flops 805437440 | bytes 8978464 | tf_op jit(solution)/shard_map/pl,skl->spk/dot_general | solution.py:49
  320.7 0.9 fusion.32
  321.6 1.6 copy.26
  323.2 0.0 reduce-scatter.5.cloned.1.call-update
  323.3 22.5 %all-gather.7.cloned.1.call-done = f32[32,8192]{1,0:T(8,128)} async-done(((f32[32,512]{1,0:T(8,128)}), f32[32,8192]{1,0:T(8,128)}) %all-gather.7.cloned.1.call-update) | async-done | bytes 1048592 | tf_op jit(solution)/shard_map/all_gather | solution.py:43
  345.7 1.3 copy.33
  347.0 0.6 gather_fusion.1
  347.6 58.2 %reduce-scatter.5.cloned.1.call-done = f32[32,512]{1,0:T(8,128)} async-done(((f32[32,8192]{1,0:T(8,128)}), f32[32,512]{1,0:T(8,128)}) %reduce-scatter.5.cloned.1.call-update) | async-done | bytes 65552 | tf_op jit(solution)/shard_map/reduce_scatter | solution.py:55
  405.8 7.2 %fusion.26 = f32[32,512]{1,0:T(8,128)S(1)} fusion(f32[32,512]{1,0:T(8,128)} %reduce-scatter.5.cloned.1.call-done, f32[8,1,512,512]{3,2,1,0:T(8,128)} %param.10, f32[8,32,512]{2,1,0:T(8,128)S(1)} %gather_fusion.1, f32[8]{0:T(128)S(1)} %compare_select_fusion.2, pred[8]{0:T(512)(128)(4,1)S(1)} %compare_and_fusion), kind=kOutput, calls=%fused_computation.20 | convolution fusion | flops 805584896 | bytes 9044008 | tf_op jit(solution)/shard_map/psk,skl->pl/dot_general | solution.py:47
  413.0 4.9 all-gather.1
  418.0 0.9 convolution_subtract_fusion.1
  418.9 0.2 fusion.82
  419.1 57.6 %psum.38 = f32[32,32]{1,0:T(8,128)S(1)} all-reduce(f32[32,32]{1,0:T(8,128)S(1)} %fusion.82), channel_id=1, replica_groups=mesh['row'=2,'col'=16] {'col'}, use_global_device_ids=true, to_apply=%region_9.13 | all-reduce | flops 1024 | bytes 8192 | tf_op jit(solution)/shard_map/psum | solution.py:12
  476.7 0.2 convolution_subtract_fusion
  476.9 0.2 fusion.83
  477.1 57.6 %psum.39 = f32[32,32]{1,0:T(8,128)S(1)} all-reduce(f32[32,32]{1,0:T(8,128)S(1)} %fusion.83), channel_id=1, replica_groups=mesh['row'=2,'col'=16] {'col'}, use_global_device_ids=true, to_apply=%region_10.14 | all-reduce | flops 1024 | bytes 8192 | tf_op jit(solution)/shard_map/psum | solution.py:12
  534.7 0.1 copy.21
  534.8 0.1 copy.22
  534.9 2.9 cholesky.81
  537.9 0.6 compare_reduce_fusion
  538.5 0.7 select_bitcast_fusion
  539.2 2.4 custom-call.9
  541.6 0.9 fusion.48
  542.5 0.6 pad_maximum_fusion
  (26 shorter events, 0.2 us)
Async XLA Ops:
  7.2 0.8 copy-start
  7.2 107.1 %all-gather.5.cloned.1.call-start = ((), (), s32[]{:S(2)}) async-start(), calls=%async_computation.2 | async-start | bytes 1114112 | tf_op jit(solution)/shard_map/all_gather | solution.py:43
  79.0 95.5 %reduce-scatter.3.cloned.1.call-start = ((), (), s32[]{:S(2)}) async-start(), calls=%async_computation.3 | async-start | bytes 1114112 | tf_op jit(solution)/shard_map/reduce_scatter | solution.py:55
  89.0 97.6 %copy-start.1 = (f32[32,512]{1,0:T(8,128)S(1)}, f32[32,512]{1,0:T(8,128)}, u32[]{:S(2)}) copy-start(f32[32,512]{1,0:T(8,128)} %fusion.54) | copy-start | bytes 196612
  89.0 97.6 %copy-start.3 = (f32[512]{0:T(512)S(1)}, f32[512]{0:T(512)}, u32[]{:S(2)}) copy-start(f32[512]{0:T(512)} %param.9) | copy-start | bytes 6148
  91.6 254.1 %all-gather.7.cloned.1.call-start = ((), (), s32[]{:S(2)}) async-start(), calls=%async_computation.4 | async-start | bytes 1114112 | tf_op jit(solution)/shard_map/all_gather | solution.py:43
  310.5 95.4 %reduce-scatter.5.cloned.1.call-start = ((), (), s32[]{:S(2)}) async-start(), calls=%async_computation.5 | async-start | bytes 1114112 | tf_op jit(solution)/shard_map/reduce_scatter | solution.py:55
  320.7 97.3 %copy-start.2 = (f32[32,512]{1,0:T(8,128)S(1)}, f32[32,512]{1,0:T(8,128)}, u32[]{:S(2)}) copy-start(f32[32,512]{1,0:T(8,128)} %fusion.51) | copy-start | bytes 196612
Sparse Core Ops, SparseCore 0:
  79.1 35.1 all-gather.4
  117.9 56.5 reduce-scatter.2
  310.6 35.0 all-gather.6
  349.2 56.5 reduce-scatter.4
